TPU v7x, 256 devices: a whole 4x4x8 slice. The times are simulated.
256 devices in a mesh: tgt: 32 (over z, y_hi, core), src: 8 (over y_lo, x).
Axes of the slice: x: 4, y: 4 (y_hi: 2, y_lo: 2; y = y_hi * 2 + y_lo), z: 8, core: 2. Of those that a mesh axis runs over, the one named last changes fastest.
Arguments:
- tgt_points: bfloat16 [3, 16384], P(None, 'tgt'), may hold values from -4 to 4
- tgt_weight: float32 [16384], P('tgt'), may hold values from 0.5 to 2
- src_points: bfloat16 [4, 3, 32768], P(None, None, ('tgt', 'src')), may hold values from -4 to 4
- src_weight: float32 [4, 32768], P(None, ('tgt', 'src')), may hold values from 0.5 to 2
- basis: float32 [4, 3, 32768], P(None, None, ('tgt', 'src')), may hold values from 0.05 to 1
- span: int32 [4, 32768], P(None, ('tgt', 'src')), may hold values from 0 to 29
- patch: int32 [4, 32768], P(None, ('tgt', 'src')), may hold values from 0 to 3
- patch_factor: float32 [4, 2, 1024], P(None, None, ('tgt', 'src')), may hold values from -1.5 to 1.5
- ctrl_weight: float32 [4, 8192], P(None, ('tgt', 'src')), may hold values from 0.5 to 2
- ctrl_coef: bfloat16 [4, 128, 8192], P(None, None, ('tgt', 'src')), may hold values from -6 to 6
- band: float32 [8, 16384], P(None, 'tgt'), may hold values from -0.5 to 0.5
- offsets: int32 [8], replicated, may hold values from -8 to 8, as said below
Outputs:
- shell_field: float32 [16384, 128], P('tgt')
Inputs may be any that keep to these rules, and one draw needn't show every extreme that they name: span of source point j is local to the 32 control points of the block j // 128. patch of source point j is local to the 4 patches of the block j // 128. offsets[0] is 8 and offsets[1] is -8.
All inputs are finite; a program needn't handle non-finite values.
Results may differ from a plain program's by a relative error of at most 0.0041.
Values may be sent and summed in bfloat16 or wider, within the bound.
No kernel may reach another device: no remote copies, remote signals or barrier semaphores. Data moves between devices by JAX's collectives and lax.ppermute only.
A program may use at most 128 MiB of HBM per device.

v0:
```python
import math
import jax
import jax.numpy as jnp
from jax import lax
from jax.sharding import PartitionSpec as P

HALO = 8
WAVE = 8.0
SMOOTH = 0.0025


def extended(block, sides, width):
    for axis, dim in sides:
        count = lax.axis_size(axis)
        forward = [(i, i + 1) for i in range(count - 1)]
        backward = [(target, source) for source, target in forward]
        low = lax.ppermute(
            lax.slice_in_dim(block, block.shape[dim] - width, None, axis=dim), axis, forward
        )
        high = lax.ppermute(lax.slice_in_dim(block, 0, width, axis=dim), axis, backward)
        block = jnp.concatenate([low, block, high], axis=dim)
    return block


def kernel_terms(targets, sources, density):
    tpos = targets.astype(jnp.float32)
    spos = sources.astype(jnp.float32)
    dist_sq = SMOOTH + (tpos[0][:, None] - spos[0][None, :]) ** 2
    dist_sq = dist_sq + (tpos[1][:, None] - spos[1][None, :]) ** 2
    dist_sq = dist_sq + (tpos[2][:, None] - spos[2][None, :]) ** 2
    dist = jnp.sqrt(dist_sq)
    kernel_re = (jnp.cos(WAVE * dist) / dist).astype(jnp.bfloat16)
    kernel_im = (jnp.sin(WAVE * dist) / dist).astype(jnp.bfloat16)
    dims = (((1,), (1,)), ((), ()))
    part_a = lax.dot_general(kernel_re, density, dims, preferred_element_type=jnp.float32)
    part_b = lax.dot_general(kernel_im, density, dims, preferred_element_type=jnp.float32)
    half = density.shape[0] // 2
    return jnp.concatenate(
        [part_a[:, :half] - part_b[:, half:], part_a[:, half:] + part_b[:, :half]], axis=1
    )


def block_density(weight, basis_rows, span_row, patch_row, factor_rows, weights_ctrl, coef_ctrl):
    count = weight.shape[0]
    fields = coef_ctrl.shape[0] // 2
    denom = jnp.zeros((count,), jnp.float32)
    numer = jnp.zeros((coef_ctrl.shape[0], count), jnp.float32)
    for basis_index in range(basis_rows.shape[0]):
        control_index = span_row + basis_index
        scaled = basis_rows[basis_index] * weights_ctrl[control_index]
        denom = denom + scaled
        numer = numer + scaled[None, :] * coef_ctrl[:, control_index].astype(jnp.float32)
    ratio = numer / denom[None, :]
    labels = jnp.arange(factor_rows.shape[1], dtype=jnp.int32)
    member = patch_row[None, :] == labels[:, None]
    factor_re = jnp.sum(jnp.where(member, factor_rows[0][:, None], 0.0), axis=0)
    factor_im = jnp.sum(jnp.where(member, factor_rows[1][:, None], 0.0), axis=0)
    ratio_re = ratio[:fields]
    ratio_im = ratio[fields:]
    dens_re = weight * (factor_re * ratio_re - factor_im * ratio_im)
    dens_im = weight * (factor_re * ratio_im + factor_im * ratio_re)
    return jnp.concatenate([dens_re, dens_im], axis=0).astype(jnp.bfloat16)


def add_kernel(carried, targets, geometry, density):
    width = geometry.shape[1]
    block_size = 1024

    def step_fn(index, inner):
        begin = index * block_size
        part_geo = lax.dynamic_slice_in_dim(geometry, begin, block_size, 1)
        part_den = lax.dynamic_slice_in_dim(density, begin, block_size, 1)
        return inner + kernel_terms(targets, part_geo, part_den)

    return lax.fori_loop(0, width // block_size, step_fn, carried)


def per_device(
    tgt_points,
    tgt_weight,
    src_points,
    src_weight,
    basis,
    span,
    patch,
    patch_factor,
    ctrl_weight,
    ctrl_coef,
    band,
    offsets,
):
    rows = tgt_points.shape[1]
    columns = ctrl_coef.shape[1]
    rounds = src_weight.shape[0]
    partial_value = jnp.zeros((rows, columns), jnp.float32)
    for section in range(rounds):
        density = block_density(
            src_weight[section],
            basis[section],
            span[section],
            patch[section],
            patch_factor[section],
            ctrl_weight[section],
            ctrl_coef[section],
        )
        geometry, gathered = (
            lax.all_gather(src_points[section], "tgt", axis=1, tiled=True),
            lax.all_gather(density, "tgt", axis=1, tiled=True),
        )
        partial_value = add_kernel(partial_value, tgt_points, geometry, gathered)
    total = lax.psum(partial_value, "src")
    source_count = rounds * src_weight.shape[1] * lax.axis_size("tgt") * lax.axis_size("src")
    scale = jnp.float32(1.0 / math.sqrt(source_count))
    potential = total * scale * tgt_weight[:, None]
    padded = extended(potential, (("tgt", 0),), HALO)
    shell_field = potential
    for diag in range(band.shape[0]):
        begin = HALO + offsets[diag]
        shifted = lax.dynamic_slice_in_dim(padded, begin, rows, 0)
        shell_field = shell_field + band[diag][:, None] * shifted
    return shell_field


def solution(mesh):
    in_specs = (
        P(None, "tgt"),
        P("tgt"),
        P(None, None, ("tgt", "src")),
        P(None, ("tgt", "src")),
        P(None, None, ("tgt", "src")),
        P(None, ("tgt", "src")),
        P(None, ("tgt", "src")),
        P(None, None, ("tgt", "src")),
        P(None, ("tgt", "src")),
        P(None, None, ("tgt", "src")),
        P(None, "tgt"),
        P(),
    )
    out_specs = P("tgt", None)
    return jax.shard_map(
        per_device, mesh=mesh, in_specs=in_specs, out_specs=out_specs, check_vma=False
    )
```

profile of v0, /device:TPU:1, one launch (start us, length us, event | category | flops | bytes accessed | tf_op | source)
XLA Modules:
  0.0 627.5 jit_solution(9285904822959095373)
XLA Ops:
  37.3 46.2 %all-gather = bf16[1,3,4096]{2,1,0:T(4,128)(2,1)S(1)} all-gather(bf16[1,3,128]{2,1,0:T(4,128)(2,1)S(1)} %copy.57), channel_id=2, replica_groups=mesh['tgt'=32,'src'=8] {'tgt'}, dimensions={2}, use_global_device_ids=true | all-gather | bytes 25344 | tf_op jit(solution)/shard_map/all_gather | solution.py:107
  83.5 36.7 %all-gather.1 = bf16[1,3,4096]{2,1,0:T(4,128)(2,1)S(1)} all-gather(bf16[1,3,128]{2,1,0:T(4,128)(2,1)S(1)} %copy.58), channel_id=3, replica_groups=mesh['tgt'=32,'src'=8] {'tgt'}, dimensions={2}, use_global_device_ids=true | all-gather | bytes 25344 | tf_op jit(solution)/shard_map/all_gather | solution.py:107
  120.2 39.6 %all-gather.2 = bf16[1,3,4096]{2,1,0:T(4,128)(2,1)S(1)} all-gather(bf16[1,3,128]{2,1,0:T(4,128)(2,1)S(1)} %copy.59), channel_id=4, replica_groups=mesh['tgt'=32,'src'=8] {'tgt'}, dimensions={2}, use_global_device_ids=true | all-gather | bytes 25344 | tf_op jit(solution)/shard_map/all_gather | solution.py:107
  159.8 36.7 %all-gather.3 = bf16[1,3,4096]{2,1,0:T(4,128)(2,1)S(1)} all-gather(bf16[1,3,128]{2,1,0:T(4,128)(2,1)S(1)} %copy.60), channel_id=5, replica_groups=mesh['tgt'=32,'src'=8] {'tgt'}, dimensions={2}, use_global_device_ids=true | all-gather | bytes 25344 | tf_op jit(solution)/shard_map/all_gather | solution.py:107
  196.5 78.8 %while.56 = (s32[]{:T(128)}, f32[512,128]{0,1:T(8,128)S(1)}, bf16[3,512]{1,0:T(4,128)(2,1)S(1)}, bf16[3,4096]{1,0:T(4,128)(2,1)S(1)}, bf16[128,4096]{1,0:T(8,128...) while((s32[]{:T(128)}, f32[512,128]{0,1:T(8,128)S(1)}, bf16[3,512]{1,0:T(4,128)(2,1)S(1)}, ...), condition=%wide.region_3.4_spmd.clone, body=%wide.region_2.3_spmd.clone.sunk | while | flops 281283584 | bytes 2713769 | solution.py:75
  196.7 9.7 %fusion.110 = f32[512,128]{0,1:T(8,128)S(1)} fusion(f32[1024]{0:T(1024)S(1)} %bitcast.278, f32[512]{0:T(512)S(1)} %bitcast.304, f32[1024]{0:T(1024)S(1)} %bitcast.280, f32[512]{0:T(512)S(1)} %bitcast.302, f32[1024]{0:T(1024)S(1)} %bitcast.276, f32[512]{0:T(512)S(1)} %bitcast.300, bf16[128,4096]{1,0:T(8,128)(2,1)} %get-tuple-element.859, ...), kind=kOutput, calls=%fused_computation.79.clone.1 | convolution fusion | flops 140509184 | bytes 542724 | tf_op jit(solution)/shard_map/while/body/eval_jaxpr/dot_general | solution.py:36
  216.3 9.7 %fusion.110 = f32[512,128]{0,1:T(8,128)S(1)} fusion(f32[1024]{0:T(1024)S(1)} %bitcast.278, f32[512]{0:T(512)S(1)} %bitcast.304, f32[1024]{0:T(1024)S(1)} %bitcast.280, f32[512]{0:T(512)S(1)} %bitcast.302, f32[1024]{0:T(1024)S(1)} %bitcast.276, f32[512]{0:T(512)S(1)} %bitcast.300, bf16[128,4096]{1,0:T(8,128)(2,1)} %get-tuple-element.859, ...), kind=kOutput, calls=%fused_computation.79.clone.1 | convolution fusion | flops 140509184 | bytes 542724 | tf_op jit(solution)/shard_map/while/body/eval_jaxpr/dot_general | solution.py:36
  235.8 9.7 %fusion.110 = f32[512,128]{0,1:T(8,128)S(1)} fusion(f32[1024]{0:T(1024)S(1)} %bitcast.278, f32[512]{0:T(512)S(1)} %bitcast.304, f32[1024]{0:T(1024)S(1)} %bitcast.280, f32[512]{0:T(512)S(1)} %bitcast.302, f32[1024]{0:T(1024)S(1)} %bitcast.276, f32[512]{0:T(512)S(1)} %bitcast.300, bf16[128,4096]{1,0:T(8,128)(2,1)} %get-tuple-element.859, ...), kind=kOutput, calls=%fused_computation.79.clone.1 | convolution fusion | flops 140509184 | bytes 542724 | tf_op jit(solution)/shard_map/while/body/eval_jaxpr/dot_general | solution.py:36
  255.4 9.7 %fusion.110 = f32[512,128]{0,1:T(8,128)S(1)} fusion(f32[1024]{0:T(1024)S(1)} %bitcast.278, f32[512]{0:T(512)S(1)} %bitcast.304, f32[1024]{0:T(1024)S(1)} %bitcast.280, f32[512]{0:T(512)S(1)} %bitcast.302, f32[1024]{0:T(1024)S(1)} %bitcast.276, f32[512]{0:T(512)S(1)} %bitcast.300, bf16[128,4096]{1,0:T(8,128)(2,1)} %get-tuple-element.859, ...), kind=kOutput, calls=%fused_computation.79.clone.1 | convolution fusion | flops 140509184 | bytes 542724 | tf_op jit(solution)/shard_map/while/body/eval_jaxpr/dot_general | solution.py:36
  275.3 78.1 %while.53 = (s32[]{:T(128)}, f32[512,128]{0,1:T(8,128)S(1)}, bf16[3,512]{1,0:T(4,128)(2,1)S(1)}, bf16[3,4096]{1,0:T(4,128)(2,1)S(1)}, bf16[128,4096]{1,0:T(8,128...) while((s32[]{:T(128)}, f32[512,128]{0,1:T(8,128)S(1)}, bf16[3,512]{1,0:T(4,128)(2,1)S(1)}, ...), condition=%wide.region_7.8_spmd, body=%wide.region_6.7_spmd.sunk | while | flops 281218048 | bytes 2713759 | solution.py:75
  275.4 9.7 %fusion.92 = f32[512,128]{0,1:T(8,128)S(1)} fusion(f32[1024]{0:T(1024)S(1)} %bitcast.284, f32[512]{0:T(512)S(1)} %bitcast.310, f32[1024]{0:T(1024)S(1)} %bitcast.286, f32[512]{0:T(512)S(1)} %bitcast.308, f32[1024]{0:T(1024)S(1)} %bitcast.282, f32[512]{0:T(512)S(1)} %bitcast.306, bf16[128,4096]{1,0:T(8,128)(2,1)} %get-tuple-element.886, ...), kind=kOutput, calls=%fused_computation.28.clone.1 | convolution fusion | flops 140509184 | bytes 542724 | tf_op jit(solution)/shard_map/while/body/eval_jaxpr/dot_general | solution.py:36
  294.9 9.7 %fusion.92 = f32[512,128]{0,1:T(8,128)S(1)} fusion(f32[1024]{0:T(1024)S(1)} %bitcast.284, f32[512]{0:T(512)S(1)} %bitcast.310, f32[1024]{0:T(1024)S(1)} %bitcast.286, f32[512]{0:T(512)S(1)} %bitcast.308, f32[1024]{0:T(1024)S(1)} %bitcast.282, f32[512]{0:T(512)S(1)} %bitcast.306, bf16[128,4096]{1,0:T(8,128)(2,1)} %get-tuple-element.886, ...), kind=kOutput, calls=%fused_computation.28.clone.1 | convolution fusion | flops 140509184 | bytes 542724 | tf_op jit(solution)/shard_map/while/body/eval_jaxpr/dot_general | solution.py:36
  314.5 9.7 %fusion.92 = f32[512,128]{0,1:T(8,128)S(1)} fusion(f32[1024]{0:T(1024)S(1)} %bitcast.284, f32[512]{0:T(512)S(1)} %bitcast.310, f32[1024]{0:T(1024)S(1)} %bitcast.286, f32[512]{0:T(512)S(1)} %bitcast.308, f32[1024]{0:T(1024)S(1)} %bitcast.282, f32[512]{0:T(512)S(1)} %bitcast.306, bf16[128,4096]{1,0:T(8,128)(2,1)} %get-tuple-element.886, ...), kind=kOutput, calls=%fused_computation.28.clone.1 | convolution fusion | flops 140509184 | bytes 542724 | tf_op jit(solution)/shard_map/while/body/eval_jaxpr/dot_general | solution.py:36
  334.0 9.7 %fusion.92 = f32[512,128]{0,1:T(8,128)S(1)} fusion(f32[1024]{0:T(1024)S(1)} %bitcast.284, f32[512]{0:T(512)S(1)} %bitcast.310, f32[1024]{0:T(1024)S(1)} %bitcast.286, f32[512]{0:T(512)S(1)} %bitcast.308, f32[1024]{0:T(1024)S(1)} %bitcast.282, f32[512]{0:T(512)S(1)} %bitcast.306, bf16[128,4096]{1,0:T(8,128)(2,1)} %get-tuple-element.886, ...), kind=kOutput, calls=%fused_computation.28.clone.1 | convolution fusion | flops 140509184 | bytes 542724 | tf_op jit(solution)/shard_map/while/body/eval_jaxpr/dot_general | solution.py:36
  353.5 78.3 %while.54 = (s32[]{:T(128)}, f32[512,128]{0,1:T(8,128)S(1)}, bf16[3,512]{1,0:T(4,128)(2,1)S(1)}, bf16[3,4096]{1,0:T(4,128)(2,1)S(1)}, bf16[128,4096]{1,0:T(8,128...) while((s32[]{:T(128)}, f32[512,128]{0,1:T(8,128)S(1)}, bf16[3,512]{1,0:T(4,128)(2,1)S(1)}, ...), condition=%wide.region_11.12_spmd, body=%wide.region_10.11_spmd.sunk | while | flops 281218048 | bytes 2713759 | solution.py:75
  373.3 9.7 %fusion.98 = f32[512,128]{0,1:T(8,128)S(1)} fusion(f32[1024]{0:T(1024)S(1)} %bitcast.290, f32[512]{0:T(512)S(1)} %bitcast.316, f32[1024]{0:T(1024)S(1)} %bitcast.292, f32[512]{0:T(512)S(1)} %bitcast.314, f32[1024]{0:T(1024)S(1)} %bitcast.288, f32[512]{0:T(512)S(1)} %bitcast.312, bf16[128,4096]{1,0:T(8,128)(2,1)} %get-tuple-element.913, ...), kind=kOutput, calls=%fused_computation.45.clone.1 | convolution fusion | flops 140509184 | bytes 542724 | tf_op jit(solution)/shard_map/while/body/eval_jaxpr/dot_general | solution.py:36
  392.8 9.7 %fusion.98 = f32[512,128]{0,1:T(8,128)S(1)} fusion(f32[1024]{0:T(1024)S(1)} %bitcast.290, f32[512]{0:T(512)S(1)} %bitcast.316, f32[1024]{0:T(1024)S(1)} %bitcast.292, f32[512]{0:T(512)S(1)} %bitcast.314, f32[1024]{0:T(1024)S(1)} %bitcast.288, f32[512]{0:T(512)S(1)} %bitcast.312, bf16[128,4096]{1,0:T(8,128)(2,1)} %get-tuple-element.913, ...), kind=kOutput, calls=%fused_computation.45.clone.1 | convolution fusion | flops 140509184 | bytes 542724 | tf_op jit(solution)/shard_map/while/body/eval_jaxpr/dot_general | solution.py:36
  412.3 9.7 %fusion.98 = f32[512,128]{0,1:T(8,128)S(1)} fusion(f32[1024]{0:T(1024)S(1)} %bitcast.290, f32[512]{0:T(512)S(1)} %bitcast.316, f32[1024]{0:T(1024)S(1)} %bitcast.292, f32[512]{0:T(512)S(1)} %bitcast.314, f32[1024]{0:T(1024)S(1)} %bitcast.288, f32[512]{0:T(512)S(1)} %bitcast.312, bf16[128,4096]{1,0:T(8,128)(2,1)} %get-tuple-element.913, ...), kind=kOutput, calls=%fused_computation.45.clone.1 | convolution fusion | flops 140509184 | bytes 542724 | tf_op jit(solution)/shard_map/while/body/eval_jaxpr/dot_general | solution.py:36
  431.8 91.2 %while.55 = (s32[]{:T(128)}, f32[512,128]{0,1:T(8,128)S(1)}, bf16[3,512]{1,0:T(4,128)(2,1)S(1)}, bf16[3,4096]{1,0:T(4,128)(2,1)S(1)}, bf16[128,4096]{1,0:T(8,128...) while((s32[]{:T(128)}, f32[512,128]{0,1:T(8,128)S(1)}, bf16[3,512]{1,0:T(4,128)(2,1)S(1)}, ...), condition=%wide.region_15.16_spmd, body=%wide.region_14.15_spmd.sunk | while | flops 281218048 | bytes 2713759 | solution.py:75
  445.0 9.7 %fusion.104 = f32[512,128]{0,1:T(8,128)S(1)} fusion(f32[1024]{0:T(1024)S(1)} %bitcast.296, f32[512]{0:T(512)S(1)} %bitcast.322, f32[1024]{0:T(1024)S(1)} %bitcast.298, f32[512]{0:T(512)S(1)} %bitcast.320, f32[1024]{0:T(1024)S(1)} %bitcast.294, f32[512]{0:T(512)S(1)} %bitcast.318, bf16[128,4096]{1,0:T(8,128)(2,1)} %get-tuple-element.940, ...), kind=kOutput, calls=%fused_computation.62.clone.1 | convolution fusion | flops 140509184 | bytes 542724 | tf_op jit(solution)/shard_map/while/body/eval_jaxpr/dot_general | solution.py:36
  464.5 9.7 %fusion.104 = f32[512,128]{0,1:T(8,128)S(1)} fusion(f32[1024]{0:T(1024)S(1)} %bitcast.296, f32[512]{0:T(512)S(1)} %bitcast.322, f32[1024]{0:T(1024)S(1)} %bitcast.298, f32[512]{0:T(512)S(1)} %bitcast.320, f32[1024]{0:T(1024)S(1)} %bitcast.294, f32[512]{0:T(512)S(1)} %bitcast.318, bf16[128,4096]{1,0:T(8,128)(2,1)} %get-tuple-element.940, ...), kind=kOutput, calls=%fused_computation.62.clone.1 | convolution fusion | flops 140509184 | bytes 542724 | tf_op jit(solution)/shard_map/while/body/eval_jaxpr/dot_general | solution.py:36
  484.1 9.7 %fusion.104 = f32[512,128]{0,1:T(8,128)S(1)} fusion(f32[1024]{0:T(1024)S(1)} %bitcast.296, f32[512]{0:T(512)S(1)} %bitcast.322, f32[1024]{0:T(1024)S(1)} %bitcast.298, f32[512]{0:T(512)S(1)} %bitcast.320, f32[1024]{0:T(1024)S(1)} %bitcast.294, f32[512]{0:T(512)S(1)} %bitcast.318, bf16[128,4096]{1,0:T(8,128)(2,1)} %get-tuple-element.940, ...), kind=kOutput, calls=%fused_computation.62.clone.1 | convolution fusion | flops 140509184 | bytes 542724 | tf_op jit(solution)/shard_map/while/body/eval_jaxpr/dot_general | solution.py:36
  503.6 9.7 %fusion.104 = f32[512,128]{0,1:T(8,128)S(1)} fusion(f32[1024]{0:T(1024)S(1)} %bitcast.296, f32[512]{0:T(512)S(1)} %bitcast.322, f32[1024]{0:T(1024)S(1)} %bitcast.298, f32[512]{0:T(512)S(1)} %bitcast.320, f32[1024]{0:T(1024)S(1)} %bitcast.294, f32[512]{0:T(512)S(1)} %bitcast.318, bf16[128,4096]{1,0:T(8,128)(2,1)} %get-tuple-element.940, ...), kind=kOutput, calls=%fused_computation.62.clone.1 | convolution fusion | flops 140509184 | bytes 542724 | tf_op jit(solution)/shard_map/while/body/eval_jaxpr/dot_general | solution.py:36
  524.0 71.3 %all-reduce.2.cloned.1.call-done = f32[512,128]{1,0:T(8,128)} async-done(((f32[512,128]{1,0:T(8,128)}), f32[512,128]{1,0:T(8,128)}) %all-reduce.2.cloned.1.call-update) | async-done | bytes 262160 | tf_op jit(solution)/shard_map/psum | solution.py:111
  (213 shorter events, 212.5 us)
Async XLA Ops:
  6.5 190.0 %all-gather.9.cloned.1.call-start = ((), (), s32[]{:S(2)}) async-start(), calls=%async_computation | async-start | bytes 1081344 | tf_op jit(solution)/shard_map/all_gather | solution.py:108
  17.7 5.0 copy-start.6
  17.7 5.0 copy-start.7
  17.7 5.0 copy-start.8
  17.7 5.1 copy-start.5
  23.6 251.7 %all-gather.11.cloned.1.call-start = ((), (), s32[]{:S(2)}) async-start(), calls=%async_computation.1 | async-start | bytes 1081344 | tf_op jit(solution)/shard_map/all_gather | solution.py:108
  26.8 326.6 %all-gather.13.cloned.1.call-start = ((), (), s32[]{:S(2)}) async-start(), calls=%async_computation.2 | async-start | bytes 1081344 | tf_op jit(solution)/shard_map/all_gather | solution.py:108
  32.7 4.5 copy-start.4
  33.0 163.5 %copy-start = (bf16[3,512]{1,0:T(4,128)(2,1)S(1)}, bf16[3,512]{1,0:T(4,128)(2,1)}, u32[]{:S(2)}) copy-start(bf16[3,512]{1,0:T(4,128)(2,1)} %param.20) | copy-start | bytes 9220
  33.9 397.9 %all-gather.15.cloned.1.call-start = ((), (), s32[]{:S(2)}) async-start(), calls=%async_computation.3 | async-start | bytes 1081344 | tf_op jit(solution)/shard_map/all_gather | solution.py:108
  37.2 558.2 %all-reduce.2.cloned.1.call-start = ((), (), s32[]{:S(2)}) async-start(), calls=%async_computation.4 | async-start | bytes 524288 | tf_op jit(solution)/shard_map/psum | solution.py:111
  431.8 92.1 %copy-start.9 = (f32[512]{0:T(512)S(1)}, f32[512]{0:T(512)}, u32[]{:S(2)}) copy-start(f32[512]{0:T(512)} %param.21) | copy-start | bytes 6148
  431.8 92.1 %copy-start.3 = (f32[8,512]{1,0:T(8,128)S(1)}, f32[8,512]{1,0:T(8,128)}, u32[]{:S(2)}) copy-start(f32[8,512]{1,0:T(8,128)} %param.30) | copy-start | bytes 49156
  523.1 85.2 %copy-start.2 = (s32[8]{0:T(128)S(1)}, s32[8]{0:T(128)}, u32[]{:S(2)}) copy-start(s32[8]{0:T(128)} %param.31) | copy-start | bytes 100
  595.3 23.9 %copy-start.1 = (f32[512,128]{1,0:T(8,128)S(1)}, f32[512,128]{1,0:T(8,128)}, u32[]{:S(2)}) copy-start(f32[512,128]{1,0:T(8,128)} %all-reduce.2.cloned.1.call-done) | copy-start | bytes 786436
  596.5 22.7 %collective-permute-start.1 = (f32[8,128]{1,0:T(8,128)S(1)}, f32[8,128]{1,0:T(8,128)S(1)}, u32[]{:S(2)}, u32[]{:S(2)}) collective-permute-start(f32[8,128]{1,0:T(8,128)S(1)} %get-tuple-element.560), channel_id=1, source_target_pairs={{8,0},{16,8},{24,16},{32,24},{40,32},{48,40},{56,48},{64,56},{72,6... | collective-permute-start | bytes 12296 | tf_op jit(solution)/shard_map/ppermute | solution.py:20
  604.0 15.2 %collective-permute-start = (f32[8,128]{1,0:T(8,128)S(1)}, f32[8,128]{1,0:T(8,128)S(1)}, u32[]{:S(2)}, u32[]{:S(2)}) collective-permute-start(f32[8,128]{1,0:T(8,128)S(1)} %get-tuple-element.559), channel_id=1, source_target_pairs={{0,8},{8,16},{16,24},{24,32},{32,40},{40,48},{48,56},{56,64},{64,7... | collective-permute-start | bytes 12296 | tf_op jit(solution)/shard_map/ppermute | solution.py:17
Sparse Core Ops, SparseCore 0:
  23.7 76.4 all-gather.8
  102.7 70.0 all-gather.10
  175.4 69.8 all-gather.12
  247.7 69.9 all-gather.14
  524.1 71.2 all-reduce.1
where the time goes:
time: 635 us; the launch traced here: 628 us
  matrix products  309 us (49%)
  blocking collectives  159 us (25%)
  waiting for transfers between devices  71.5 us (11%)
  local copies, waits for them, and re-layouts  28.2 us (4%)
  between operations  24.2 us (4%)
  loops' own time  15.1 us (2%)
  starting transfers between devices  11.9 us (2%)
  other arithmetic  8.44 us (1%)
    all_gather x4, blocking collectives, per_device(): lax.all_gather(src_points[section], 'tgt', axis=1, tiled=True)  159 us
    dot_general x16, matrix products, kernel_terms(): lax.dot_general(kernel_im, density, dims, preferred_element_type=jnp.floa...  155 us
    dot_general x16, matrix products, kernel_terms(): lax.dot_general(kernel_re, density, dims, preferred_element_type=jnp.floa...  154 us
    psum x1, waiting for transfers between devices, per_device(): total = lax.psum(partial_value, 'src')  71.3 us
    another operation x4, loops' own time, add_kernel(): return lax.fori_loop(0, width // block_size, step_fn, carried)  15.1 us
    gather x12, local copies, waits for them, and re-layouts, block_density(): scaled = basis_rows[basis_index] * weights_ctrl[control_index]  14.7 us
  transfers between devices with their start and end apart: 7, of which 1 were waited for; matrix products, arithmetic and copies ran while one was open for 39% of the time, Pallas kernels for 0%

commit v1 on v0

--- a/solution.py
+++ b/solution.py
@@ -103,8 +103,11 @@
             ctrl_weight[section],
             ctrl_coef[section],
         )
+        _serve_task = lambda obj, net_axis: jnp.concatenate(
+            lax.all_to_all(jnp.stack(lax.axis_size(net_axis) * [obj]), net_axis, 0, 0), axis=1
+        )
         geometry, gathered = (
-            lax.all_gather(src_points[section], "tgt", axis=1, tiled=True),
+            _serve_task(src_points[section], "tgt"),
             lax.all_gather(density, "tgt", axis=1, tiled=True),
         )
         partial_value = add_kernel(partial_value, tgt_points, geometry, gathered)

time: 635 us -> 585 us (0.921)
  blocking collectives: 159 us -> 0 us
  waiting for transfers between devices: 71.5 us -> 120 us
  starting transfers between devices: 11.9 us -> 44.9 us
  loops' own time: 15.1 us -> 40.1 us
    all_gather x4 -> x0, blocking collectives: 159 us -> none  [per_device(): lax.all_gather(src_points[section], 'tgt', axis=1, tiled=True)]
    all_gather x4, waiting for transfers between devices: 0.06 us -> 38.5 us  [per_device(): lax.all_gather(density, 'tgt', axis=1, tiled=True)]
    all_to_all x0 -> x4, starting transfers between devices: none -> 33 us  [per_device(): lax.all_to_all(jnp.stack(lax.axis_size(net_axis) * [obj]), net_axis, 0, 0)]
    another operation x4, loops' own time: 15.1 us -> 40.1 us  [add_kernel(): return lax.fori_loop(0, width // block_size, step_fn, carried)]
  transfers between devices with their start and end apart: 7 -> 11, of which waited for: 1 -> 3; matrix products, arithmetic and copies ran while one was open for 39% -> 43% of each run, Pallas kernels for 0% -> 0%
where the time goes in v1:
time: 585 us; the launch traced here: 577 us
  matrix products  309 us (53%)
  waiting for transfers between devices  120 us (21%)
  starting transfers between devices  44.9 us (8%)
  loops' own time  40.1 us (7%)
  local copies, waits for them, and re-layouts  30.7 us (5%)
  between operations  24.1 us (4%)
  other arithmetic  8.42 us (1%)
    dot_general x16, matrix products, kernel_terms(): lax.dot_general(kernel_im, density, dims, preferred_element_type=jnp.floa...  155 us
    dot_general x16, matrix products, kernel_terms(): lax.dot_general(kernel_re, density, dims, preferred_element_type=jnp.floa...  154 us
    psum x1, waiting for transfers between devices, per_device(): total = lax.psum(partial_value, 'src')  74.9 us
    another operation x4, loops' own time, add_kernel(): return lax.fori_loop(0, width // block_size, step_fn, carried)  40.1 us
    all_gather x4, waiting for transfers between devices, per_device(): lax.all_gather(density, 'tgt', axis=1, tiled=True)  38.5 us
    all_to_all x4, starting transfers between devices, per_device(): lax.all_to_all(jnp.stack(lax.axis_size(net_axis) * [obj]), net_axis, 0, 0)  33 us
    gather x12, local copies, waits for them, and re-layouts, block_density(): scaled = basis_rows[basis_index] * weights_ctrl[control_index]  14.7 us
  transfers between devices with their start and end apart: 11, of which 3 were waited for; matrix products, arithmetic and copies ran while one was open for 43% of the time, Pallas kernels for 0%

profile of v1, /device:TPU:1, one launch (start us, length us, event | category | flops | bytes accessed | tf_op | source)
XLA Modules:
  0.0 577.2 jit_solution(1185861934704539967)
XLA Ops:
  34.6 12.7 %all-to-all-start = ((bf16[32,3,128]{2,1,0:T(4,128)(2,1)}), bf16[32,3,128]{2,1,0:T(4,128)(2,1)S(1)}, u32[]{:S(2)}, u32[]{:S(2)}) async-start(bf16[32,3,128]{2,1,0:T(4,128)(2,1)} %stack.12), calls=%async_computation | async-start | bytes 65536 | tf_op jit(solution)/shard_map/all_to_all | solution.py:107
  61.6 38.5 %all-gather.5.cloned.1.call-done = bf16[128,4096]{1,0:T(8,128)(2,1)} async-done(((bf16[128,128]{1,0:T(8,128)(2,1)}), bf16[128,4096]{1,0:T(8,128)(2,1)}) %all-gather.5.cloned.1.call-update) | async-done | bytes 1048592 | tf_op jit(solution)/shard_map/all_gather | solution.py:111
  100.1 91.2 %while.56 = (s32[]{:T(128)}, f32[512,128]{0,1:T(8,128)S(1)}, bf16[3,512]{1,0:T(4,128)(2,1)S(1)}, bf16[3,4096]{1,0:T(4,128)(2,1)S(1)}, bf16[128,4096]{1,0:T(8,128...) while((s32[]{:T(128)}, f32[512,128]{0,1:T(8,128)S(1)}, bf16[3,512]{1,0:T(4,128)(2,1)S(1)}, ...), condition=%wide.region_3.4_spmd.clone, body=%wide.region_2.3_spmd.clone.sunk | while | flops 281283584 | bytes 2713769 | solution.py:75
  100.3 9.7 %fusion.110 = f32[512,128]{0,1:T(8,128)S(1)} fusion(f32[1024]{0:T(1024)S(1)} %bitcast.298, f32[512]{0:T(512)S(1)} %bitcast.324, f32[1024]{0:T(1024)S(1)} %bitcast.300, f32[512]{0:T(512)S(1)} %bitcast.322, f32[1024]{0:T(1024)S(1)} %bitcast.296, f32[512]{0:T(512)S(1)} %bitcast.320, bf16[128,4096]{1,0:T(8,128)(2,1)} %get-tuple-element.879, ...), kind=kOutput, calls=%fused_computation.79.clone.1 | convolution fusion | flops 140509184 | bytes 542724 | tf_op jit(solution)/shard_map/while/body/eval_jaxpr/dot_general | solution.py:36
  119.9 9.7 %fusion.110 = f32[512,128]{0,1:T(8,128)S(1)} fusion(f32[1024]{0:T(1024)S(1)} %bitcast.298, f32[512]{0:T(512)S(1)} %bitcast.324, f32[1024]{0:T(1024)S(1)} %bitcast.300, f32[512]{0:T(512)S(1)} %bitcast.322, f32[1024]{0:T(1024)S(1)} %bitcast.296, f32[512]{0:T(512)S(1)} %bitcast.320, bf16[128,4096]{1,0:T(8,128)(2,1)} %get-tuple-element.879, ...), kind=kOutput, calls=%fused_computation.79.clone.1 | convolution fusion | flops 140509184 | bytes 542724 | tf_op jit(solution)/shard_map/while/body/eval_jaxpr/dot_general | solution.py:36
  139.4 9.7 %fusion.110 = f32[512,128]{0,1:T(8,128)S(1)} fusion(f32[1024]{0:T(1024)S(1)} %bitcast.298, f32[512]{0:T(512)S(1)} %bitcast.324, f32[1024]{0:T(1024)S(1)} %bitcast.300, f32[512]{0:T(512)S(1)} %bitcast.322, f32[1024]{0:T(1024)S(1)} %bitcast.296, f32[512]{0:T(512)S(1)} %bitcast.320, bf16[128,4096]{1,0:T(8,128)(2,1)} %get-tuple-element.879, ...), kind=kOutput, calls=%fused_computation.79.clone.1 | convolution fusion | flops 140509184 | bytes 542724 | tf_op jit(solution)/shard_map/while/body/eval_jaxpr/dot_general | solution.py:36
  159.0 9.7 %fusion.110 = f32[512,128]{0,1:T(8,128)S(1)} fusion(f32[1024]{0:T(1024)S(1)} %bitcast.298, f32[512]{0:T(512)S(1)} %bitcast.324, f32[1024]{0:T(1024)S(1)} %bitcast.300, f32[512]{0:T(512)S(1)} %bitcast.322, f32[1024]{0:T(1024)S(1)} %bitcast.296, f32[512]{0:T(512)S(1)} %bitcast.320, bf16[128,4096]{1,0:T(8,128)(2,1)} %get-tuple-element.879, ...), kind=kOutput, calls=%fused_computation.79.clone.1 | convolution fusion | flops 140509184 | bytes 542724 | tf_op jit(solution)/shard_map/while/body/eval_jaxpr/dot_general | solution.py:36
  198.4 91.0 %while.53 = (s32[]{:T(128)}, f32[512,128]{0,1:T(8,128)S(1)}, bf16[3,512]{1,0:T(4,128)(2,1)S(1)}, bf16[3,4096]{1,0:T(4,128)(2,1)S(1)}, bf16[128,4096]{1,0:T(8,128...) while((s32[]{:T(128)}, f32[512,128]{0,1:T(8,128)S(1)}, bf16[3,512]{1,0:T(4,128)(2,1)S(1)}, ...), condition=%wide.region_7.8_spmd, body=%wide.region_6.7_spmd.sunk | while | flops 281218048 | bytes 2713759 | solution.py:75
  198.5 9.7 %fusion.92 = f32[512,128]{0,1:T(8,128)S(1)} fusion(f32[1024]{0:T(1024)S(1)} %bitcast.304, f32[512]{0:T(512)S(1)} %bitcast.330, f32[1024]{0:T(1024)S(1)} %bitcast.306, f32[512]{0:T(512)S(1)} %bitcast.328, f32[1024]{0:T(1024)S(1)} %bitcast.302, f32[512]{0:T(512)S(1)} %bitcast.326, bf16[128,4096]{1,0:T(8,128)(2,1)} %get-tuple-element.906, ...), kind=kOutput, calls=%fused_computation.28.clone.1 | convolution fusion | flops 140509184 | bytes 542724 | tf_op jit(solution)/shard_map/while/body/eval_jaxpr/dot_general | solution.py:36
  218.0 9.7 %fusion.92 = f32[512,128]{0,1:T(8,128)S(1)} fusion(f32[1024]{0:T(1024)S(1)} %bitcast.304, f32[512]{0:T(512)S(1)} %bitcast.330, f32[1024]{0:T(1024)S(1)} %bitcast.306, f32[512]{0:T(512)S(1)} %bitcast.328, f32[1024]{0:T(1024)S(1)} %bitcast.302, f32[512]{0:T(512)S(1)} %bitcast.326, bf16[128,4096]{1,0:T(8,128)(2,1)} %get-tuple-element.906, ...), kind=kOutput, calls=%fused_computation.28.clone.1 | convolution fusion | flops 140509184 | bytes 542724 | tf_op jit(solution)/shard_map/while/body/eval_jaxpr/dot_general | solution.py:36
  237.6 9.7 %fusion.92 = f32[512,128]{0,1:T(8,128)S(1)} fusion(f32[1024]{0:T(1024)S(1)} %bitcast.304, f32[512]{0:T(512)S(1)} %bitcast.330, f32[1024]{0:T(1024)S(1)} %bitcast.306, f32[512]{0:T(512)S(1)} %bitcast.328, f32[1024]{0:T(1024)S(1)} %bitcast.302, f32[512]{0:T(512)S(1)} %bitcast.326, bf16[128,4096]{1,0:T(8,128)(2,1)} %get-tuple-element.906, ...), kind=kOutput, calls=%fused_computation.28.clone.1 | convolution fusion | flops 140509184 | bytes 542724 | tf_op jit(solution)/shard_map/while/body/eval_jaxpr/dot_general | solution.py:36
  257.1 9.7 %fusion.92 = f32[512,128]{0,1:T(8,128)S(1)} fusion(f32[1024]{0:T(1024)S(1)} %bitcast.304, f32[512]{0:T(512)S(1)} %bitcast.330, f32[1024]{0:T(1024)S(1)} %bitcast.306, f32[512]{0:T(512)S(1)} %bitcast.328, f32[1024]{0:T(1024)S(1)} %bitcast.302, f32[512]{0:T(512)S(1)} %bitcast.326, bf16[128,4096]{1,0:T(8,128)(2,1)} %get-tuple-element.906, ...), kind=kOutput, calls=%fused_computation.28.clone.1 | convolution fusion | flops 140509184 | bytes 542724 | tf_op jit(solution)/shard_map/while/body/eval_jaxpr/dot_general | solution.py:36
  290.1 9.8 %all-to-all-start.3 = ((bf16[32,3,128]{2,1,0:T(4,128)(2,1)}), bf16[32,3,128]{2,1,0:T(4,128)(2,1)S(1)}, u32[]{:S(2)}, u32[]{:S(2)}) async-start(bf16[32,3,128]{2,1,0:T(4,128)(2,1)} %stack.15), calls=%async_computation.3 | async-start | bytes 65536 | tf_op jit(solution)/shard_map/all_to_all | solution.py:107
  299.9 78.1 %while.54 = (s32[]{:T(128)}, f32[512,128]{0,1:T(8,128)S(1)}, bf16[3,512]{1,0:T(4,128)(2,1)S(1)}, bf16[3,4096]{1,0:T(4,128)(2,1)S(1)}, bf16[128,4096]{1,0:T(8,128...) while((s32[]{:T(128)}, f32[512,128]{0,1:T(8,128)S(1)}, bf16[3,512]{1,0:T(4,128)(2,1)S(1)}, ...), condition=%wide.region_11.12_spmd, body=%wide.region_10.11_spmd.sunk | while | flops 281218048 | bytes 2713759 | solution.py:75
  300.0 9.7 %fusion.98 = f32[512,128]{0,1:T(8,128)S(1)} fusion(f32[1024]{0:T(1024)S(1)} %bitcast.310, f32[512]{0:T(512)S(1)} %bitcast.336, f32[1024]{0:T(1024)S(1)} %bitcast.312, f32[512]{0:T(512)S(1)} %bitcast.334, f32[1024]{0:T(1024)S(1)} %bitcast.308, f32[512]{0:T(512)S(1)} %bitcast.332, bf16[128,4096]{1,0:T(8,128)(2,1)} %get-tuple-element.933, ...), kind=kOutput, calls=%fused_computation.45.clone.1 | convolution fusion | flops 140509184 | bytes 542724 | tf_op jit(solution)/shard_map/while/body/eval_jaxpr/dot_general | solution.py:36
  319.5 9.7 %fusion.98 = f32[512,128]{0,1:T(8,128)S(1)} fusion(f32[1024]{0:T(1024)S(1)} %bitcast.310, f32[512]{0:T(512)S(1)} %bitcast.336, f32[1024]{0:T(1024)S(1)} %bitcast.312, f32[512]{0:T(512)S(1)} %bitcast.334, f32[1024]{0:T(1024)S(1)} %bitcast.308, f32[512]{0:T(512)S(1)} %bitcast.332, bf16[128,4096]{1,0:T(8,128)(2,1)} %get-tuple-element.933, ...), kind=kOutput, calls=%fused_computation.45.clone.1 | convolution fusion | flops 140509184 | bytes 542724 | tf_op jit(solution)/shard_map/while/body/eval_jaxpr/dot_general | solution.py:36
  339.0 9.7 %fusion.98 = f32[512,128]{0,1:T(8,128)S(1)} fusion(f32[1024]{0:T(1024)S(1)} %bitcast.310, f32[512]{0:T(512)S(1)} %bitcast.336, f32[1024]{0:T(1024)S(1)} %bitcast.312, f32[512]{0:T(512)S(1)} %bitcast.334, f32[1024]{0:T(1024)S(1)} %bitcast.308, f32[512]{0:T(512)S(1)} %bitcast.332, bf16[128,4096]{1,0:T(8,128)(2,1)} %get-tuple-element.933, ...), kind=kOutput, calls=%fused_computation.45.clone.1 | convolution fusion | flops 140509184 | bytes 542724 | tf_op jit(solution)/shard_map/while/body/eval_jaxpr/dot_general | solution.py:36
  358.5 9.7 %fusion.98 = f32[512,128]{0,1:T(8,128)S(1)} fusion(f32[1024]{0:T(1024)S(1)} %bitcast.310, f32[512]{0:T(512)S(1)} %bitcast.336, f32[1024]{0:T(1024)S(1)} %bitcast.312, f32[512]{0:T(512)S(1)} %bitcast.334, f32[1024]{0:T(1024)S(1)} %bitcast.308, f32[512]{0:T(512)S(1)} %bitcast.332, bf16[128,4096]{1,0:T(8,128)(2,1)} %get-tuple-element.933, ...), kind=kOutput, calls=%fused_computation.45.clone.1 | convolution fusion | flops 140509184 | bytes 542724 | tf_op jit(solution)/shard_map/while/body/eval_jaxpr/dot_general | solution.py:36
  378.1 91.2 %while.55 = (s32[]{:T(128)}, f32[512,128]{0,1:T(8,128)S(1)}, bf16[3,512]{1,0:T(4,128)(2,1)S(1)}, bf16[3,4096]{1,0:T(4,128)(2,1)S(1)}, bf16[128,4096]{1,0:T(8,128...) while((s32[]{:T(128)}, f32[512,128]{0,1:T(8,128)S(1)}, bf16[3,512]{1,0:T(4,128)(2,1)S(1)}, ...), condition=%wide.region_15.16_spmd, body=%wide.region_14.15_spmd.sunk | while | flops 281218048 | bytes 2713759 | solution.py:75
  391.2 9.7 %fusion.104 = f32[512,128]{0,1:T(8,128)S(1)} fusion(f32[1024]{0:T(1024)S(1)} %bitcast.316, f32[512]{0:T(512)S(1)} %bitcast.342, f32[1024]{0:T(1024)S(1)} %bitcast.318, f32[512]{0:T(512)S(1)} %bitcast.340, f32[1024]{0:T(1024)S(1)} %bitcast.314, f32[512]{0:T(512)S(1)} %bitcast.338, bf16[128,4096]{1,0:T(8,128)(2,1)} %get-tuple-element.960, ...), kind=kOutput, calls=%fused_computation.62.clone.1 | convolution fusion | flops 140509184 | bytes 542724 | tf_op jit(solution)/shard_map/while/body/eval_jaxpr/dot_general | solution.py:36
  410.8 9.7 %fusion.104 = f32[512,128]{0,1:T(8,128)S(1)} fusion(f32[1024]{0:T(1024)S(1)} %bitcast.316, f32[512]{0:T(512)S(1)} %bitcast.342, f32[1024]{0:T(1024)S(1)} %bitcast.318, f32[512]{0:T(512)S(1)} %bitcast.340, f32[1024]{0:T(1024)S(1)} %bitcast.314, f32[512]{0:T(512)S(1)} %bitcast.338, bf16[128,4096]{1,0:T(8,128)(2,1)} %get-tuple-element.960, ...), kind=kOutput, calls=%fused_computation.62.clone.1 | convolution fusion | flops 140509184 | bytes 542724 | tf_op jit(solution)/shard_map/while/body/eval_jaxpr/dot_general | solution.py:36
  430.3 9.7 %fusion.104 = f32[512,128]{0,1:T(8,128)S(1)} fusion(f32[1024]{0:T(1024)S(1)} %bitcast.316, f32[512]{0:T(512)S(1)} %bitcast.342, f32[1024]{0:T(1024)S(1)} %bitcast.318, f32[512]{0:T(512)S(1)} %bitcast.340, f32[1024]{0:T(1024)S(1)} %bitcast.314, f32[512]{0:T(512)S(1)} %bitcast.338, bf16[128,4096]{1,0:T(8,128)(2,1)} %get-tuple-element.960, ...), kind=kOutput, calls=%fused_computation.62.clone.1 | convolution fusion | flops 140509184 | bytes 542724 | tf_op jit(solution)/shard_map/while/body/eval_jaxpr/dot_general | solution.py:36
  449.8 9.7 %fusion.104 = f32[512,128]{0,1:T(8,128)S(1)} fusion(f32[1024]{0:T(1024)S(1)} %bitcast.316, f32[512]{0:T(512)S(1)} %bitcast.342, f32[1024]{0:T(1024)S(1)} %bitcast.318, f32[512]{0:T(512)S(1)} %bitcast.340, f32[1024]{0:T(1024)S(1)} %bitcast.314, f32[512]{0:T(512)S(1)} %bitcast.338, bf16[128,4096]{1,0:T(8,128)(2,1)} %get-tuple-element.960, ...), kind=kOutput, calls=%fused_computation.62.clone.1 | convolution fusion | flops 140509184 | bytes 542724 | tf_op jit(solution)/shard_map/while/body/eval_jaxpr/dot_general | solution.py:36
  470.2 74.9 %all-reduce.2.cloned.1.call-done = f32[512,128]{1,0:T(8,128)} async-done(((f32[512,128]{1,0:T(8,128)}), f32[512,128]{1,0:T(8,128)}) %all-reduce.2.cloned.1.call-update) | async-done | bytes 262160 | tf_op jit(solution)/shard_map/psum | solution.py:114
  (221 shorter events, 222.0 us)
Async XLA Ops:
  6.5 93.5 %all-gather.5.cloned.1.call-start = ((), (), s32[]{:S(2)}) async-start(), calls=%async_computation.4 | async-start | bytes 1081344 | tf_op jit(solution)/shard_map/all_gather | solution.py:111
  17.7 5.0 copy-start.6
  17.7 5.0 copy-start.7
  17.7 5.0 copy-start.8
  17.7 5.1 copy-start.5
  23.6 174.8 %all-gather.7.cloned.1.call-start = ((), (), s32[]{:S(2)}) async-start(), calls=%async_computation.5 | async-start | bytes 1081344 | tf_op jit(solution)/shard_map/all_gather | solution.py:111
  26.8 273.1 %all-gather.9.cloned.1.call-start = ((), (), s32[]{:S(2)}) async-start(), calls=%async_computation.6 | async-start | bytes 1081344 | tf_op jit(solution)/shard_map/all_gather | solution.py:111
  29.5 4.4 copy-start.4
  33.2 66.9 %copy-start = (bf16[3,512]{1,0:T(4,128)(2,1)S(1)}, bf16[3,512]{1,0:T(4,128)(2,1)}, u32[]{:S(2)}) copy-start(bf16[3,512]{1,0:T(4,128)(2,1)} %param.20) | copy-start | bytes 9220
  34.6 22.4 %all-to-all-start = ((bf16[32,3,128]{2,1,0:T(4,128)(2,1)}), bf16[32,3,128]{2,1,0:T(4,128)(2,1)S(1)}, u32[]{:S(2)}, u32[]{:S(2)}) async-start(bf16[32,3,128]{2,1,0:T(4,128)(2,1)} %stack.12), calls=%async_computation | async-start | bytes 65536 | tf_op jit(solution)/shard_map/all_to_all | solution.py:107
  47.3 330.7 %all-gather.11.cloned.1.call-start = ((), (), s32[]{:S(2)}) async-start(), calls=%async_computation.7 | async-start | bytes 1081344 | tf_op jit(solution)/shard_map/all_gather | solution.py:111
  57.6 133.7 %all-to-all-start.1 = ((bf16[32,3,128]{2,1,0:T(4,128)(2,1)}), bf16[32,3,128]{2,1,0:T(4,128)(2,1)S(1)}, u32[]{:S(2)}, u32[]{:S(2)}) async-start(bf16[32,3,128]{2,1,0:T(4,128)(2,1)} %stack.13), calls=%async_computation.1 | async-start | bytes 65536 | tf_op jit(solution)/shard_map/all_to_all | solution.py:107
  191.9 97.5 %all-to-all-start.2 = ((bf16[32,3,128]{2,1,0:T(4,128)(2,1)}), bf16[32,3,128]{2,1,0:T(4,128)(2,1)S(1)}, u32[]{:S(2)}, u32[]{:S(2)}) async-start(bf16[32,3,128]{2,1,0:T(4,128)(2,1)} %stack.14), calls=%async_computation.2 | async-start | bytes 65536 | tf_op jit(solution)/shard_map/all_to_all | solution.py:107
  290.1 88.0 %all-to-all-start.3 = ((bf16[32,3,128]{2,1,0:T(4,128)(2,1)}), bf16[32,3,128]{2,1,0:T(4,128)(2,1)S(1)}, u32[]{:S(2)}, u32[]{:S(2)}) async-start(bf16[32,3,128]{2,1,0:T(4,128)(2,1)} %stack.15), calls=%async_computation.3 | async-start | bytes 65536 | tf_op jit(solution)/shard_map/all_to_all | solution.py:107
  299.8 245.3 %all-reduce.2.cloned.1.call-start = ((), (), s32[]{:S(2)}) async-start(), calls=%async_computation.8 | async-start | bytes 524288 | tf_op jit(solution)/shard_map/psum | solution.py:114
  378.0 92.1 %copy-start.9 = (f32[512]{0:T(512)S(1)}, f32[512]{0:T(512)}, u32[]{:S(2)}) copy-start(f32[512]{0:T(512)} %param.21) | copy-start | bytes 6148
  378.1 92.1 %copy-start.3 = (f32[8,512]{1,0:T(8,128)S(1)}, f32[8,512]{1,0:T(8,128)}, u32[]{:S(2)}) copy-start(f32[8,512]{1,0:T(8,128)} %param.30) | copy-start | bytes 49156
  469.3 88.8 %copy-start.2 = (s32[8]{0:T(128)S(1)}, s32[8]{0:T(128)}, u32[]{:S(2)}) copy-start(s32[8]{0:T(128)} %param.31) | copy-start | bytes 100
  545.2 23.8 %copy-start.1 = (f32[512,128]{1,0:T(8,128)S(1)}, f32[512,128]{1,0:T(8,128)}, u32[]{:S(2)}) copy-start(f32[512,128]{1,0:T(8,128)} %all-reduce.2.cloned.1.call-done) | copy-start | bytes 786436
  546.3 22.5 %collective-permute-start.1 = (f32[8,128]{1,0:T(8,128)S(1)}, f32[8,128]{1,0:T(8,128)S(1)}, u32[]{:S(2)}, u32[]{:S(2)}) collective-permute-start(f32[8,128]{1,0:T(8,128)S(1)} %get-tuple-element.580), channel_id=1, source_target_pairs={{8,0},{16,8},{24,16},{32,24},{40,32},{48,40},{56,48},{64,56},{72,6... | collective-permute-start | bytes 12296 | tf_op jit(solution)/shard_map/ppermute | solution.py:20
  553.8 15.1 %collective-permute-start = (f32[8,128]{1,0:T(8,128)S(1)}, f32[8,128]{1,0:T(8,128)S(1)}, u32[]{:S(2)}, u32[]{:S(2)}) collective-permute-start(f32[8,128]{1,0:T(8,128)S(1)} %get-tuple-element.579), channel_id=1, source_target_pairs={{0,8},{8,16},{16,24},{24,32},{32,40},{40,48},{48,56},{56,64},{64,7... | collective-permute-start | bytes 12296 | tf_op jit(solution)/shard_map/ppermute | solution.py:17
Sparse Core Ops, SparseCore 0:
  23.7 76.3 all-gather.4
  102.6 69.9 all-gather.6
  175.2 69.9 all-gather.8
  247.6 69.9 all-gather.10
  470.3 74.8 all-reduce.1
